TPU v7x, 128 devices: a whole 4x4x4 slice. The times are simulated.
128 devices in a mesh: row: 4 (over x_hi, core), col: 32 (over y, x_lo, z).
Axes of the slice: x: 4 (x_hi: 2, x_lo: 2; x = x_hi * 2 + x_lo), y: 4, z: 4, core: 2. Of those that a mesh axis runs over, the one named last changes fastest.
Arguments:
- tokens: bfloat16 [49152, 2048], P('col', 'row'), may hold values from -6 to 6
- in_weight: float32 [2048, 6144], P(('row', 'col')), may hold values from -0.125 to 0.125
- out_weight: float32 [2048, 2048], P(('row', 'col')), may hold values from -0.125 to 0.125
- beta_weight: float32 [2048, 16], replicated, may hold values from -0.25 to 0.25
- conv_weight: float32 [4, 6144], P(None, 'row'), may hold values from -2.5 to 2.5
- conv_prior: bfloat16 [96, 3, 6144], P('col', None, 'row'), may hold values from -6 to 6
- head_gain: float32 [2048], P('row'), may hold values from 0.1 to 1.9
- state_pool: float32 [192, 16, 128, 128], P('col', 'row'), may hold values from -2.5 to 2.5
- state_index: int32 [96, 16], P('col', 'row'), may hold values from 0 to 5
- lengths: int32 [96], P('col'), may hold values from 1 to 512, 36864 in all
- page_table: int32 [96, 4, 2], P('col'), may hold values from 0 to 31, as said below
Outputs:
- server_in: bfloat16 [2048, 6144], P('row', 'col')
- server_out: bfloat16 [2048, 2048], P('row', 'col')
- layer_out: bfloat16 [49152, 2048], P('col', 'row')
- final_state: float32 [96, 16, 128, 128], P('col', 'row')
- page_cache: bfloat16 [384, 128, 2, 2048], P('col', None, None, 'row')
Inputs may be any that keep to these rules, and one draw needn't show every extreme that they name: `lengths`: one prompt has all 512 tokens live. `state_index`: which of its own index of col's 6 stored states a prompt and head continues. page_table[p, g, 0] is the index of col that keeps page g of prompt p and page_table[p, g, 1] its slot there, below 12; every slot of every index of col gets exactly one page; the prompts of one index of col send at most 1 pages to any one index of col, and exactly 1 to some.
All inputs are finite; a program needn't handle non-finite values. No bound on the sum of `lengths` on one device may be relied on, other than what follows from the above.
Results may differ from a plain program's by a relative error of at most 0.029.
Values may be sent and summed in bfloat16 or wider, within the bound.
No kernel may reach another device: no remote copies, remote signals or barrier semaphores. Data moves between devices by JAX's collectives and lax.ppermute only.
A program may use at most 128 MiB of HBM per device.

v0:
```python
import jax
import jax.numpy as jnp
from jax import lax
from jax.sharding import PartitionSpec as P

DK = 128
STRETCH = 64
CONV = 4
SEQ = 512
PAGE = 128
PAGES_SEQ = 4
HIGHEST = lax.Precision.HIGHEST


def delta_block(carry_state, block_data):
    query_unit, key_unit, values, beta_rates = block_data
    width_c = beta_rates.shape[1]
    width_k = key_unit.shape[2]
    strict_lower = jnp.tril(jnp.ones((width_c, width_c), jnp.float32), -1)
    causal = jnp.tril(jnp.ones((width_c, width_c), jnp.float32))
    gram_matrix = jnp.einsum("bik,bjk->bij", key_unit, key_unit, precision=HIGHEST)
    system = (
        jnp.eye(width_c, dtype=jnp.float32) + beta_rates[:, :, None] * gram_matrix * strict_lower
    )
    right_side = jnp.concatenate([key_unit, values], axis=2) * beta_rates[:, :, None]
    solved = jax.scipy.linalg.solve_triangular(system, right_side, lower=True, unit_diagonal=True)
    weighted = solved[:, :, :width_k]
    corrected = solved[:, :, width_k:] - jnp.einsum(
        "bck,bkv->bcv", weighted, carry_state, precision=HIGHEST
    )
    scores = jnp.einsum("bik,bjk->bij", query_unit, key_unit, precision=HIGHEST) * causal
    output = jnp.einsum("bck,bkv->bcv", query_unit, carry_state, precision=HIGHEST) + jnp.einsum(
        "bij,bjv->biv", scores, corrected, precision=HIGHEST
    )
    carry_state = carry_state + jnp.einsum("bck,bcv->bkv", key_unit, corrected, precision=HIGHEST)
    return (carry_state, output)


def delta_scan(query_unit, key_unit, values, beta_rates, initial, block_len):
    batch_n = query_unit.shape[0]
    length_all = query_unit.shape[1]
    num_blocks = length_all // block_len

    def to_blocks(tensor):
        shaped = tensor.reshape((batch_n, num_blocks, block_len) + tensor.shape[2:])
        return jnp.moveaxis(shaped, 1, 0)

    last_state, outputs = lax.scan(
        delta_block,
        initial,
        (to_blocks(query_unit), to_blocks(key_unit), to_blocks(values), to_blocks(beta_rates)),
    )
    outputs = jnp.moveaxis(outputs, 0, 1).reshape(batch_n, length_all, -1)
    return (last_state, outputs)


def unit_rows(tensor):
    return tensor * lax.rsqrt(jnp.sum(tensor * tensor, axis=-1, keepdims=True) + 1e-06)


def local(
    tokens,
    in_weight,
    out_weight,
    beta_weight,
    conv_weight,
    conv_prior,
    head_gain,
    state_pool,
    state_index,
    lengths,
    page_table,
):
    row_count = lax.axis_size("row")
    col_count = lax.axis_size("col")
    row_id = lax.axis_index("row")
    local_tokens = tokens.shape[0]
    feature_span = tokens.shape[1]
    head_group = state_index.shape[1]
    head_width = 3 * DK
    prompts_here = lengths.shape[0]
    trainer_in = in_weight.astype(jnp.bfloat16)
    server_in, server_out = (
        lax.all_to_all(trainer_in, "col", split_axis=1, concat_axis=0, tiled=True),
        lax.all_to_all(
            out_weight.astype(jnp.bfloat16), "col", split_axis=1, concat_axis=0, tiled=True
        ),
    )
    beta_cast = beta_weight.astype(jnp.bfloat16)
    wide_in, wide_out = (
        lax.all_gather(server_in, "col", axis=1, tiled=True),
        lax.all_gather(server_out, "col", axis=1, tiled=True),
    )
    columns = wide_in
    product = jnp.dot(tokens, columns, preferred_element_type=jnp.float32)
    qkv_sum = lax.psum_scatter(
        product.reshape(local_tokens, lax.axis_size("row") * head_group, head_width)
        .transpose(1, 0, 2)
        .astype(jnp.bfloat16),
        "row",
        scatter_dimension=0,
        tiled=True,
    )
    beta_rows = lax.dynamic_slice_in_dim(beta_cast, row_id * feature_span, feature_span, 0)
    beta_term = jnp.dot(tokens, beta_rows, preferred_element_type=jnp.float32).T
    beta_sum = lax.psum_scatter(
        beta_term.astype(jnp.bfloat16), "row", scatter_dimension=0, tiled=True
    ).astype(jnp.float32)
    projected = qkv_sum.reshape(head_group, prompts_here, SEQ, head_width)
    prior_rows = conv_prior.reshape(prompts_here, CONV - 1, head_group, head_width).transpose(
        2, 0, 1, 3
    )
    padded = jnp.concatenate(
        [prior_rows.astype(jnp.float32), projected.astype(jnp.float32)], axis=2
    )
    taps_all = conv_weight.reshape(CONV, head_group, head_width)
    conv_sum = jnp.zeros(projected.shape, jnp.float32)
    for tap_id in range(CONV):
        conv_sum = (
            conv_sum + taps_all[tap_id][:, None, None, :] * padded[:, :, tap_id : tap_id + SEQ]
        )
    activated = jax.nn.silu(conv_sum).reshape(head_group * prompts_here, SEQ, 3, DK)
    query_unit = unit_rows(activated[:, :, 0])
    key_unit = unit_rows(activated[:, :, 1])
    values = activated[:, :, 2]
    live_mask = (jnp.arange(SEQ, dtype=jnp.int32)[None, :] < lengths[:, None]).astype(jnp.float32)
    live_batch = jnp.broadcast_to(live_mask[None], (head_group, prompts_here, SEQ)).reshape(
        head_group * prompts_here, SEQ
    )
    beta_rates = live_batch * jax.nn.sigmoid(beta_sum.reshape(head_group * prompts_here, SEQ))
    picked = state_pool[state_index, jnp.arange(head_group, dtype=jnp.int32)[None, :]]
    initial = picked.transpose(1, 0, 2, 3).reshape(head_group * prompts_here, DK, DK)
    last_state, outputs = delta_scan(query_unit, key_unit, values, beta_rates, initial, STRETCH)
    outputs = outputs * live_batch[:, :, None]
    normed = outputs.reshape(head_group, prompts_here, SEQ, DK)
    normed = (
        normed
        * lax.rsqrt(jnp.mean(normed * normed, axis=3, keepdims=True) + 1e-05)
        * head_gain.reshape(head_group, 1, 1, DK)
    )
    flat_heads = (
        normed.astype(jnp.bfloat16).transpose(1, 2, 0, 3).reshape(local_tokens, head_group * DK)
    )
    out_span = wide_out.shape[1] // row_count
    columns = wide_out
    product = jnp.dot(flat_heads, columns, preferred_element_type=jnp.float32)
    layer_out = (
        lax.psum_scatter(
            product.reshape(local_tokens, lax.axis_size("row") * 1, out_span)
            .transpose(1, 0, 2)
            .astype(jnp.bfloat16),
            "row",
            scatter_dimension=0,
            tiled=True,
        )
        .astype(jnp.float32)[0]
        .astype(jnp.bfloat16)
    )
    final_state = last_state.reshape(head_group, prompts_here, DK, DK).transpose(1, 0, 2, 3)
    keep_mask = live_batch[:, :, None]
    kept_pairs = jnp.stack([key_unit * keep_mask, values * keep_mask], axis=0).reshape(
        2, head_group, prompts_here, SEQ, DK
    )
    page_rows = (
        kept_pairs.transpose(2, 3, 0, 1, 4)
        .reshape(prompts_here * PAGES_SEQ, PAGE, 2, head_group * DK)
        .astype(jnp.bfloat16)
    )
    pages_dev = page_rows.shape[0]
    capacity = max(1, 2 * pages_dev // col_count)
    targets = page_table[:, :, 0].reshape(-1)
    slot_ids = page_table[:, :, 1].reshape(-1)
    order_ids = jnp.arange(pages_dev, dtype=jnp.int32)
    earlier = (targets[:, None] == targets[None, :]) & (order_ids[None, :] < order_ids[:, None])
    positions = targets * capacity + jnp.sum(earlier.astype(jnp.int32), axis=1)
    outgoing = (
        jnp.zeros((col_count * capacity,) + page_rows.shape[1:], jnp.bfloat16)
        .at[positions]
        .set(page_rows)
    )
    slot_send = jnp.full((col_count * capacity,), pages_dev, jnp.int32).at[positions].set(slot_ids)
    arrived, arrived_slots = (
        lax.all_to_all(outgoing, "col", split_axis=0, concat_axis=0, tiled=True),
        lax.all_to_all(slot_send, "col", split_axis=0, concat_axis=0, tiled=True),
    )
    page_cache = (
        jnp.zeros(page_rows.shape, jnp.bfloat16).at[arrived_slots].set(arrived, mode="drop")
    )
    return (server_in, server_out, layer_out, final_state, page_cache)


def solution(mesh):
    return jax.shard_map(
        local,
        mesh=mesh,
        in_specs=(
            P("col", "row"),
            P(("row", "col"), None),
            P(("row", "col"), None),
            P(),
            P(None, "row"),
            P("col", None, "row"),
            P("row"),
            P("col", "row", None, None),
            P("col", "row"),
            P("col"),
            P("col", None, None),
        ),
        out_specs=(
            P("row", "col"),
            P("row", "col"),
            P("col", "row"),
            P("col", "row", None, None),
            P("col", None, None, "row"),
        ),
        check_vma=False,
    )
```

profile of v0, /device:TPU:16, one launch (start us, length us, event | category | flops | bytes accessed | tf_op | source)
XLA Modules:
  0.0 1226.2 jit_solution(3627169898886624098)
XLA Ops:
  8.8 16.4 %all_to_all.55 = bf16[16,32,192]{2,0,1:T(8,128)(2,1)S(1)} all-to-all(bf16[16,32,192]{2,0,1:T(8,128)(2,1)S(1)} %copy.123), channel_id=1, replica_groups=mesh['row'=4,'col'=32] {'col'}, dimensions={1} | all-to-all | bytes 393216 | tf_op jit(solution)/shard_map/all_to_all | solution.py:84
  26.1 144.7 %all-gather.3.cloned.1.call-done = bf16[512,6144]{0,1:T(8,128)(2,1)} async-done(((bf16[512,192]{0,1:T(8,128)(2,1)}), bf16[512,6144]{0,1:T(8,128)(2,1)}) %all-gather.3.cloned.1.call-update) | async-done | bytes 6291472 | tf_op jit(solution)/shard_map/all_gather | solution.py:91
  170.8 15.9 %convolution_convert_fusion = bf16[1536,6144]{1,0:T(8,128)(2,1)} fusion(bf16[1536,512]{1,0:T(8,128)(2,1)S(1)} %copy-done, bf16[512,6144]{0,1:T(8,128)(2,1)} %all-gather.3.cloned.1.call-done), kind=kOutput, calls=%fused_computation.43 | convolution fusion | flops 9673113600 | bytes 26738688 | tf_op jit(solution)/shard_map/dot_general | solution.py:95
  186.7 18.3 %copy.164 = bf16[192,16,8,384]{3,2,0,1:T(8,128)(2,1)} copy(bf16[192,16,8,384]{3,2,1,0:T(8,128)(2,1)} %bitcast.161) | data formatting | bytes 37748736 | tf_op jit(solution)/shard_map/convert_element_type | solution.py:99
  207.0 25.2 %all-to-all-start.1 = ((bf16[32,2,512]{2,1,0:T(2,128)(2,1)}), bf16[32,2,512]{2,1,0:T(2,128)(2,1)S(1)}, u32[]{:S(2)}, u32[]{:S(2)}) async-start(bf16[32,2,512]{2,1,0:T(2,128)(2,1)} %reshape.338), calls=%async_computation.1 | async-start | bytes 131072 | tf_op jit(solution)/shard_map/all_to_all | solution.py:85
  234.8 13.6 %all-reduce = bf16[16,1536]{1,0:T(8,128)(2,1)S(1)} all-reduce(bf16[16,1536]{1,0:T(8,128)(2,1)S(1)} %convolution_convert_fusion.1), channel_id=3, replica_groups=mesh['row'=4,'col'=32] {'row'}, use_global_device_ids=true, to_apply=%region_3.4.clone | all-reduce | flops 24576 | bytes 98304
  252.5 116.9 %reduce-scatter.3.cloned.1.call-done = bf16[4,1536,384]{2,1,0:T(8,128)(2,1)} async-done(((bf16[16,1536,384]{2,1,0:T(8,128)(2,1)}), bf16[4,1536,384]{2,1,0:T(8,128)(2,1)}) %reduce-scatter.3.cloned.1.call-update) | async-done | bytes 4718608 | tf_op jit(solution)/shard_map/reduce_scatter | solution.py:96
  369.3 3.2 convert.14
  372.6 7.4 divide_multiply_fusion
  380.0 9.7 copy.129
  389.6 8.1 multiply_reduce_fusion
  397.8 3.5 copy.130
  401.4 3.6 copy.132
  405.0 3.6 copy.131
  408.6 3.8 multiply_bitcast_fusion.1
  414.5 554.7 %while.12 = (s32[]{:T(128)}, f32[12,128,128]{2,1,0:T(8,128)S(1)}, f32[8,12,64,128]{3,2,0,1:T(8,128)}, f32[8,12,64,128]{3,2,0,1:T(8,128)}, f32[8,12,64]{2,0,1:T(8...) while((s32[]{:T(128)}, f32[12,128,128]{2,1,0:T(8,128)S(1)}, ...), condition=%wide.region_5.6_spmd, body=%wide.region_4.5_spmd.sunk | while | flops 831590464 | bytes 12349789 | solution.py:48
  416.7 59.0 %custom-call.8 = f32[12,1,64,64]{2,3,1,0:T(8,128)S(1)} custom-call(f32[12,1,64,64]{3,2,1,0:T(8,128)S(1)} %fusion.93), custom_call_target="InvertDiagBlocksLowerTriangular" | custom-call | tf_op jit(solution)/shard_map/while/body/eval_jaxpr/jit(_solve_triangular)/vmap()/triangular_solve | solution.py:26
  479.8 2.6 fusion.97
  486.0 59.0 %custom-call.8 = f32[12,1,64,64]{2,3,1,0:T(8,128)S(1)} custom-call(f32[12,1,64,64]{3,2,1,0:T(8,128)S(1)} %fusion.93), custom_call_target="InvertDiagBlocksLowerTriangular" | custom-call | tf_op jit(solution)/shard_map/while/body/eval_jaxpr/jit(_solve_triangular)/vmap()/triangular_solve | solution.py:26
  549.1 2.6 fusion.97
  555.4 59.0 %custom-call.8 = f32[12,1,64,64]{2,3,1,0:T(8,128)S(1)} custom-call(f32[12,1,64,64]{3,2,1,0:T(8,128)S(1)} %fusion.93), custom_call_target="InvertDiagBlocksLowerTriangular" | custom-call | tf_op jit(solution)/shard_map/while/body/eval_jaxpr/jit(_solve_triangular)/vmap()/triangular_solve | solution.py:26
  618.5 2.6 fusion.97
  624.7 59.0 %custom-call.8 = f32[12,1,64,64]{2,3,1,0:T(8,128)S(1)} custom-call(f32[12,1,64,64]{3,2,1,0:T(8,128)S(1)} %fusion.93), custom_call_target="InvertDiagBlocksLowerTriangular" | custom-call | tf_op jit(solution)/shard_map/while/body/eval_jaxpr/jit(_solve_triangular)/vmap()/triangular_solve | solution.py:26
  687.8 2.6 fusion.97
  694.0 59.0 %custom-call.8 = f32[12,1,64,64]{2,3,1,0:T(8,128)S(1)} custom-call(f32[12,1,64,64]{3,2,1,0:T(8,128)S(1)} %fusion.93), custom_call_target="InvertDiagBlocksLowerTriangular" | custom-call | tf_op jit(solution)/shard_map/while/body/eval_jaxpr/jit(_solve_triangular)/vmap()/triangular_solve | solution.py:26
  757.1 2.6 fusion.97
  763.4 59.0 %custom-call.8 = f32[12,1,64,64]{2,3,1,0:T(8,128)S(1)} custom-call(f32[12,1,64,64]{3,2,1,0:T(8,128)S(1)} %fusion.93), custom_call_target="InvertDiagBlocksLowerTriangular" | custom-call | tf_op jit(solution)/shard_map/while/body/eval_jaxpr/jit(_solve_triangular)/vmap()/triangular_solve | solution.py:26
  826.5 2.6 fusion.97
  832.7 59.0 %custom-call.8 = f32[12,1,64,64]{2,3,1,0:T(8,128)S(1)} custom-call(f32[12,1,64,64]{3,2,1,0:T(8,128)S(1)} %fusion.93), custom_call_target="InvertDiagBlocksLowerTriangular" | custom-call | tf_op jit(solution)/shard_map/while/body/eval_jaxpr/jit(_solve_triangular)/vmap()/triangular_solve | solution.py:26
  895.8 2.6 fusion.97
  902.0 59.0 %custom-call.8 = f32[12,1,64,64]{2,3,1,0:T(8,128)S(1)} custom-call(f32[12,1,64,64]{3,2,1,0:T(8,128)S(1)} %fusion.93), custom_call_target="InvertDiagBlocksLowerTriangular" | custom-call | tf_op jit(solution)/shard_map/while/body/eval_jaxpr/jit(_solve_triangular)/vmap()/triangular_solve | solution.py:26
  965.1 2.6 fusion.97
  969.2 3.4 fusion.32
  972.8 2.6 fusion.33
  978.6 8.2 convert_bitcast_fusion
  989.3 7.6 all-to-all-start.2
  997.2 5.3 copy.142
  1002.5 4.9 copy.143
  1007.4 9.9 multiply_convert_fusion.1
  1017.4 3.9 maximum_bitcast_fusion
  1021.3 5.7 reshape.308
  1027.1 3.9 copy.144
  1030.9 4.2 broadcast_in_dim.32
  1035.1 8.4 scatter_fusion
  1043.5 8.3 all-to-all-start.3
  1053.5 139.6 %all-to-all-done.3 = bf16[32,128,2,512]{3,1,2,0:T(8,128)(2,1)} async-done(((bf16[32,128,2,512]{3,1,2,0:T(8,128)(2,1)}), bf16[32,128,2,512]{3,1,2,0:T(8,128)(2,1)}, u32[]{:S(2)}, u32[]{:S(2)}) %all-to-all-start.3) | async-done | bytes 8388640 | tf_op jit(solution)/shard_map/all_to_all | solution.py:183
  1195.2 17.7 %scatter_fusion.1 = bf16[12,128,2,512]{3,1,2,0:T(8,128)(2,1)} fusion(bf16[12,128,2,512]{3,1,2,0:T(8,128)(2,1)} %broadcast_in_dim.25, s32[32]{0:T(128)S(1)} %fusion.41, bf16[32,128,2,512]{3,1,2,0:T(8,128)(2,1)} %all-to-all-done.3), kind=kCustom, calls=%fused_computation.3 | custom fusion | bytes 25165952 | tf_op jit(solution)/shard_map/scatter | solution.py:187
  1212.8 6.8 copy.148
  (198 shorter events, 83.6 us)
Async XLA Ops:
  7.2 163.6 %copy-start = (bf16[1536,512]{1,0:T(8,128)(2,1)S(1)}, bf16[1536,512]{1,0:T(8,128)(2,1)}, u32[]{:S(2)}) copy-start(bf16[1536,512]{1,0:T(8,128)(2,1)} %param.13) | copy-start | bytes 4718596
  7.2 163.6 %all-gather.3.cloned.1.call-start = ((), (), s32[]{:S(2)}) async-start(), calls=%async_computation.6 | async-start | bytes 6488064 | tf_op jit(solution)/shard_map/all_gather | solution.py:91
  26.1 343.3 %reduce-scatter.3.cloned.1.call-start = ((), (), s32[]{:S(2)}) async-start(), calls=%async_computation.7 | async-start | bytes 23592960 | tf_op jit(solution)/shard_map/reduce_scatter | solution.py:96
  205.0 0.9 copy-start.3
  205.0 27.3 %copy-start.10 = (u32[128]{0:T(128)S(1)}, u32[128]{0:T(128)}, u32[]{:S(2)}) copy-start(u32[128]{0:T(128)} %constant.92) | copy-start | bytes 1540
  205.0 43.5 %copy-start.9 = (s32[3]{0:T(128)S(1)}, s32[3]{0:T(128)}, u32[]{:S(2)}) copy-start(s32[3]{0:T(128)} %param.22) | copy-start | bytes 40
  205.0 43.7 %copy-start.8 = (s32[3,4]{1,0:T(4,128)S(1)}, s32[3,4]{1,0:T(4,128)}, u32[]{:S(2)}) copy-start(s32[3,4]{1,0:T(4,128)} %param.21) | copy-start | bytes 148
  205.9 42.9 %copy-start.5 = (f32[4,1536]{1,0:T(4,128)S(1)}, f32[4,1536]{1,0:T(4,128)}, u32[]{:S(2)}) copy-start(f32[4,1536]{1,0:T(4,128)} %param.17) | copy-start | bytes 73732
  205.9 43.0 %copy-start.4 = (bf16[3,3,1536]{2,1,0:T(4,128)(2,1)S(1)}, bf16[3,3,1536]{2,1,0:T(4,128)(2,1)}, u32[]{:S(2)}) copy-start(bf16[3,3,1536]{2,1,0:T(4,128)(2,1)} %param.18) | copy-start | bytes 82948
  207.0 44.6 %all-to-all-start.1 = ((bf16[32,2,512]{2,1,0:T(2,128)(2,1)}), bf16[32,2,512]{2,1,0:T(2,128)(2,1)S(1)}, u32[]{:S(2)}, u32[]{:S(2)}) async-start(bf16[32,2,512]{2,1,0:T(2,128)(2,1)} %reshape.338), calls=%async_computation.1 | async-start | bytes 131072 | tf_op jit(solution)/shard_map/all_to_all | solution.py:85
  232.2 746.4 %all-gather.5.cloned.1.call-start = ((), (), s32[]{:S(2)}) async-start(), calls=%async_computation.8 | async-start | bytes 2162688 | tf_op jit(solution)/shard_map/all_gather | solution.py:92
  252.4 967.2 %reduce-scatter.5.cloned.1.call-start = ((), (), s32[]{:S(2)}) async-start(), calls=%async_computation.9 | async-start | bytes 7864320 | tf_op jit(solution)/shard_map/reduce_scatter | solution.py:148
  408.6 3.8 copy-start.2
  969.2 3.6 copy-start.7
  986.8 0.7 copy-start.6
  989.3 54.2 %all-to-all-start.2 = ((s32[32,1,1]{2,1,0:T(1,128)}), s32[32,1,1]{2,1,0:T(1,128)S(1)}, u32[]{:S(2)}, u32[]{:S(2)}) async-start(s32[32,1,1]{2,1,0:T(1,128)} %copy.140), calls=%async_computation.4 | async-start | bytes 32768 | tf_op jit(solution)/shard_map/all_to_all | solution.py:184
  1043.5 149.6 %all-to-all-start.3 = ((bf16[32,128,2,512]{3,1,2,0:T(8,128)(2,1)}), bf16[32,128,2,512]{3,1,2,0:T(8,128)(2,1)}, u32[]{:S(2)}, u32[]{:S(2)}) async-start(bf16[32,128,2,512]{3,1,2,0:T(8,128)(2,1)} %scatter_fusion), calls=%async_computation.5 | async-start | bytes 16777216 | tf_op jit(solution)/shard_map/all_to_all | solution.py:183
  1195.2 24.5 %copy-start.1 = (bf16[1536,512]{1,0:T(8,128)(2,1)S(1)}, bf16[1536,512]{1,0:T(8,128)(2,1)}, u32[]{:S(2)}) copy-start(bf16[1536,512]{1,0:T(8,128)(2,1)} %param.13) | copy-start | bytes 4718596
Sparse Core Ops, SparseCore 0:
  26.2 144.5 all-gather.2
  205.2 164.0 reduce-scatter.2
  371.7 135.9 all-gather.4
  987.0 64.7 reduce-scatter.4
where the time goes:
time: 1230 us
  other arithmetic  520 us (42%)
  waiting for transfers between devices  401 us (33%)
  local copies, waits for them, and re-layouts  122 us (10%)
  matrix products  96.3 us (8%)
  starting transfers between devices  41.4 us (3%)
  blocking collectives  30 us (2%)
  between operations  14.8 us (1%)
    another operation x32, other arithmetic, delta_block(): jax.scipy.linalg.solve_triangular(system, right_side, lower=True, unit_di...  473 us
    all_gather x1, waiting for transfers between devices, local(): lax.all_gather(server_in, 'col', axis=1, tiled=True)  145 us
    all_to_all x1, waiting for transfers between devices, local(): lax.all_to_all(outgoing, 'col', split_axis=0, concat_axis=0, tiled=True)  140 us
    reduce_scatter x1, waiting for transfers between devices, local(): lax.psum_scatter(product.reshape(local_tokens, lax.axis_size('row') * hea...  117 us
    all_to_all x1, starting transfers between devices, local(): lax.all_to_all(out_weight.astype(jnp.bfloat16), 'col', split_axis=1, conc...  25.2 us
  transfers between devices with their start and end apart: 7, of which 3 were waited for; matrix products, arithmetic and copies ran while one was open for 56% of the time, Pallas kernels for 0%

commit v1 on v0

--- a/solution.py
+++ b/solution.py
@@ -10,6 +10,13 @@
 PAGE = 128
 PAGES_SEQ = 4
 HIGHEST = lax.Precision.HIGHEST
+
+
+def trade_parts(x, mesh_axis, split, join):
+    size = lax.axis_size(mesh_axis)
+    shards = jnp.stack(jnp.split(x, size, axis=split), axis=0)
+    shards = lax.all_to_all(shards, mesh_axis, split_axis=0, concat_axis=0)
+    return jnp.concatenate(shards, axis=join)
 
 
 def delta_block(carry_state, block_data):
@@ -82,9 +89,7 @@
     trainer_in = in_weight.astype(jnp.bfloat16)
     server_in, server_out = (
         lax.all_to_all(trainer_in, "col", split_axis=1, concat_axis=0, tiled=True),
-        lax.all_to_all(
-            out_weight.astype(jnp.bfloat16), "col", split_axis=1, concat_axis=0, tiled=True
-        ),
+        trade_parts(out_weight.astype(jnp.bfloat16), "col", 1, 0),
     )
     beta_cast = beta_weight.astype(jnp.bfloat16)
     wide_in, wide_out = (

time: 1230 us -> 1230 us (level)
  no operation moved by 1% of the time
where the time goes in v1:
time: 1230 us
  other arithmetic  520 us (42%)
  waiting for transfers between devices  400 us (33%)
  local copies, waits for them, and re-layouts  123 us (10%)
  matrix products  96.3 us (8%)
  starting transfers between devices  41.4 us (3%)
  blocking collectives  30 us (2%)
  between operations  14.8 us (1%)
    another operation x32, other arithmetic, delta_block(): jax.scipy.linalg.solve_triangular(system, right_side, lower=True, unit_di...  473 us
    all_gather x1, waiting for transfers between devices, local(): lax.all_gather(server_in, 'col', axis=1, tiled=True)  145 us
    all_to_all x1, waiting for transfers between devices, local(): lax.all_to_all(outgoing, 'col', split_axis=0, concat_axis=0, tiled=True)  140 us
    reduce_scatter x1, waiting for transfers between devices, local(): lax.psum_scatter(product.reshape(local_tokens, lax.axis_size('row') * hea...  116 us
    all_to_all x1, starting transfers between devices, trade_parts(): shards = lax.all_to_all(shards, mesh_axis, split_axis=0, concat_axis=0)  25.2 us
  transfers between devices with their start and end apart: 7, of which 3 were waited for; matrix products, arithmetic and copies ran while one was open for 56% of the time, Pallas kernels for 0%

profile of v1, /device:TPU:16, one launch (start us, length us, event | category | flops | bytes accessed | tf_op | source)
XLA Modules:
  0.0 1226.2 jit_solution(13301100050469628550)
XLA Ops:
  8.8 16.4 %all_to_all.41 = bf16[16,32,192]{2,0,1:T(8,128)(2,1)S(1)} all-to-all(bf16[16,32,192]{2,0,1:T(8,128)(2,1)S(1)} %copy.119), channel_id=1, replica_groups=mesh['row'=4,'col'=32] {'col'}, dimensions={1} | all-to-all | bytes 393216 | tf_op jit(solution)/shard_map/all_to_all | solution.py:91
  26.1 144.7 %all-gather.3.cloned.1.call-done = bf16[512,6144]{0,1:T(8,128)(2,1)} async-done(((bf16[512,192]{0,1:T(8,128)(2,1)}), bf16[512,6144]{0,1:T(8,128)(2,1)}) %all-gather.3.cloned.1.call-update) | async-done | bytes 6291472 | tf_op jit(solution)/shard_map/all_gather | solution.py:96
  170.8 15.9 %convolution_convert_fusion = bf16[1536,6144]{1,0:T(8,128)(2,1)} fusion(bf16[1536,512]{1,0:T(8,128)(2,1)S(1)} %copy-done, bf16[512,6144]{0,1:T(8,128)(2,1)} %all-gather.3.cloned.1.call-done), kind=kOutput, calls=%fused_computation.43 | convolution fusion | flops 9673113600 | bytes 26738688 | tf_op jit(solution)/shard_map/dot_general | solution.py:100
  186.7 18.3 %copy.158 = bf16[192,16,8,384]{3,2,0,1:T(8,128)(2,1)} copy(bf16[192,16,8,384]{3,2,1,0:T(8,128)(2,1)} %bitcast.283) | data formatting | bytes 37748736 | tf_op jit(solution)/shard_map/convert_element_type | solution.py:104
  208.2 25.2 %all-to-all-start.1 = ((bf16[32,2,512]{2,1,0:T(2,128)(2,1)}), bf16[32,2,512]{2,1,0:T(2,128)(2,1)S(1)}, u32[]{:S(2)}, u32[]{:S(2)}) async-start(bf16[32,2,512]{2,1,0:T(2,128)(2,1)} %reshape.339), calls=%async_computation.1 | async-start | bytes 131072 | tf_op jit(solution)/shard_map/all_to_all | solution.py:18
  236.0 13.6 %all-reduce = bf16[16,1536]{1,0:T(8,128)(2,1)S(1)} all-reduce(bf16[16,1536]{1,0:T(8,128)(2,1)S(1)} %convolution_convert_fusion.1), channel_id=3, replica_groups=mesh['row'=4,'col'=32] {'row'}, use_global_device_ids=true, to_apply=%region_3.4.clone | all-reduce | flops 24576 | bytes 98304
  253.6 115.7 %reduce-scatter.3.cloned.1.call-done = bf16[4,1536,384]{2,1,0:T(8,128)(2,1)} async-done(((bf16[16,1536,384]{2,1,0:T(8,128)(2,1)}), bf16[4,1536,384]{2,1,0:T(8,128)(2,1)}) %reduce-scatter.3.cloned.1.call-update) | async-done | bytes 4718608 | tf_op jit(solution)/shard_map/reduce_scatter | solution.py:101
  369.4 3.2 convert.14
  372.6 7.4 divide_multiply_fusion
  380.0 9.7 copy.124
  389.7 8.1 multiply_reduce_fusion
  397.8 3.5 copy.125
  401.5 3.6 copy.127
  405.0 3.6 copy.126
  408.6 3.8 multiply_bitcast_fusion.1
  414.5 554.7 %while.12 = (s32[]{:T(128)}, f32[12,128,128]{2,1,0:T(8,128)S(1)}, f32[8,12,64,128]{3,2,0,1:T(8,128)}, f32[8,12,64,128]{3,2,0,1:T(8,128)}, f32[8,12,64]{2,0,1:T(8...) while((s32[]{:T(128)}, f32[12,128,128]{2,1,0:T(8,128)S(1)}, ...), condition=%wide.region_5.6_spmd, body=%wide.region_4.5_spmd.sunk | while | flops 831590464 | bytes 12349789 | solution.py:55
  416.7 59.0 %custom-call.10 = f32[12,1,64,64]{2,3,1,0:T(8,128)S(1)} custom-call(f32[12,1,64,64]{3,2,1,0:T(8,128)S(1)} %fusion.93), custom_call_target="InvertDiagBlocksLowerTriangular" | custom-call | tf_op jit(solution)/shard_map/while/body/eval_jaxpr/jit(_solve_triangular)/vmap()/triangular_solve | solution.py:33
  479.8 2.6 fusion.97
  486.0 59.0 %custom-call.10 = f32[12,1,64,64]{2,3,1,0:T(8,128)S(1)} custom-call(f32[12,1,64,64]{3,2,1,0:T(8,128)S(1)} %fusion.93), custom_call_target="InvertDiagBlocksLowerTriangular" | custom-call | tf_op jit(solution)/shard_map/while/body/eval_jaxpr/jit(_solve_triangular)/vmap()/triangular_solve | solution.py:33
  549.2 2.6 fusion.97
  555.4 59.0 %custom-call.10 = f32[12,1,64,64]{2,3,1,0:T(8,128)S(1)} custom-call(f32[12,1,64,64]{3,2,1,0:T(8,128)S(1)} %fusion.93), custom_call_target="InvertDiagBlocksLowerTriangular" | custom-call | tf_op jit(solution)/shard_map/while/body/eval_jaxpr/jit(_solve_triangular)/vmap()/triangular_solve | solution.py:33
  618.5 2.6 fusion.97
  624.7 59.0 %custom-call.10 = f32[12,1,64,64]{2,3,1,0:T(8,128)S(1)} custom-call(f32[12,1,64,64]{3,2,1,0:T(8,128)S(1)} %fusion.93), custom_call_target="InvertDiagBlocksLowerTriangular" | custom-call | tf_op jit(solution)/shard_map/while/body/eval_jaxpr/jit(_solve_triangular)/vmap()/triangular_solve | solution.py:33
  687.8 2.6 fusion.97
  694.0 59.0 %custom-call.10 = f32[12,1,64,64]{2,3,1,0:T(8,128)S(1)} custom-call(f32[12,1,64,64]{3,2,1,0:T(8,128)S(1)} %fusion.93), custom_call_target="InvertDiagBlocksLowerTriangular" | custom-call | tf_op jit(solution)/shard_map/while/body/eval_jaxpr/jit(_solve_triangular)/vmap()/triangular_solve | solution.py:33
  757.2 2.6 fusion.97
  763.4 59.0 %custom-call.10 = f32[12,1,64,64]{2,3,1,0:T(8,128)S(1)} custom-call(f32[12,1,64,64]{3,2,1,0:T(8,128)S(1)} %fusion.93), custom_call_target="InvertDiagBlocksLowerTriangular" | custom-call | tf_op jit(solution)/shard_map/while/body/eval_jaxpr/jit(_solve_triangular)/vmap()/triangular_solve | solution.py:33
  826.5 2.6 fusion.97
  832.7 59.0 %custom-call.10 = f32[12,1,64,64]{2,3,1,0:T(8,128)S(1)} custom-call(f32[12,1,64,64]{3,2,1,0:T(8,128)S(1)} %fusion.93), custom_call_target="InvertDiagBlocksLowerTriangular" | custom-call | tf_op jit(solution)/shard_map/while/body/eval_jaxpr/jit(_solve_triangular)/vmap()/triangular_solve | solution.py:33
  895.8 2.6 fusion.97
  902.0 59.0 %custom-call.10 = f32[12,1,64,64]{2,3,1,0:T(8,128)S(1)} custom-call(f32[12,1,64,64]{3,2,1,0:T(8,128)S(1)} %fusion.93), custom_call_target="InvertDiagBlocksLowerTriangular" | custom-call | tf_op jit(solution)/shard_map/while/body/eval_jaxpr/jit(_solve_triangular)/vmap()/triangular_solve | solution.py:33
  965.2 2.6 fusion.97
  969.2 3.4 fusion.32
  972.8 2.6 fusion.33
  978.6 8.2 convert_bitcast_fusion
  989.3 7.6 all-to-all-start.2
  997.3 5.2 copy.137
  1002.5 4.9 copy.138
  1007.4 10.0 multiply_convert_fusion.1
  1017.4 3.9 maximum_bitcast_fusion
  1021.3 5.7 reshape.309
  1027.1 3.9 copy.139
  1030.9 4.2 broadcast_in_dim.32
  1035.1 8.4 scatter_fusion
  1043.5 8.4 all-to-all-start.3
  1053.5 139.6 %all-to-all-done.3 = bf16[32,128,2,512]{3,1,2,0:T(8,128)(2,1)} async-done(((bf16[32,128,2,512]{3,1,2,0:T(8,128)(2,1)}), bf16[32,128,2,512]{3,1,2,0:T(8,128)(2,1)}, u32[]{:S(2)}, u32[]{:S(2)}) %all-to-all-start.3) | async-done | bytes 8388640 | tf_op jit(solution)/shard_map/all_to_all | solution.py:188
  1195.2 17.7 %scatter_fusion.1 = bf16[12,128,2,512]{3,1,2,0:T(8,128)(2,1)} fusion(bf16[12,128,2,512]{3,1,2,0:T(8,128)(2,1)} %broadcast_in_dim.25, s32[32]{0:T(128)S(1)} %fusion.41, bf16[32,128,2,512]{3,1,2,0:T(8,128)(2,1)} %all-to-all-done.3), kind=kCustom, calls=%fused_computation.3 | custom fusion | bytes 25165952 | tf_op jit(solution)/shard_map/scatter | solution.py:192
  1212.9 6.8 copy.143
  (228 shorter events, 84.7 us)
Async XLA Ops:
  7.2 163.6 %copy-start = (bf16[1536,512]{1,0:T(8,128)(2,1)S(1)}, bf16[1536,512]{1,0:T(8,128)(2,1)}, u32[]{:S(2)}) copy-start(bf16[1536,512]{1,0:T(8,128)(2,1)} %param.13) | copy-start | bytes 4718596
  7.2 163.6 %all-gather.3.cloned.1.call-start = ((), (), s32[]{:S(2)}) async-start(), calls=%async_computation.6 | async-start | bytes 6488064 | tf_op jit(solution)/shard_map/all_gather | solution.py:96
  26.1 343.3 %reduce-scatter.3.cloned.1.call-start = ((), (), s32[]{:S(2)}) async-start(), calls=%async_computation.7 | async-start | bytes 23592960 | tf_op jit(solution)/shard_map/reduce_scatter | solution.py:101
  205.0 0.9 copy-start.3
  205.0 28.5 %copy-start.10 = (u32[128]{0:T(128)S(1)}, u32[128]{0:T(128)}, u32[]{:S(2)}) copy-start(u32[128]{0:T(128)} %constant.92) | copy-start | bytes 1540
  205.0 44.8 %copy-start.9 = (s32[3]{0:T(128)S(1)}, s32[3]{0:T(128)}, u32[]{:S(2)}) copy-start(s32[3]{0:T(128)} %param.22) | copy-start | bytes 40
  205.0 44.9 %copy-start.8 = (s32[3,4]{1,0:T(4,128)S(1)}, s32[3,4]{1,0:T(4,128)}, u32[]{:S(2)}) copy-start(s32[3,4]{1,0:T(4,128)} %param.21) | copy-start | bytes 148
  205.0 44.9 %copy-start.5 = (f32[4,1536]{1,0:T(4,128)S(1)}, f32[4,1536]{1,0:T(4,128)}, u32[]{:S(2)}) copy-start(f32[4,1536]{1,0:T(4,128)} %param.17) | copy-start | bytes 73732
  205.1 45.1 %copy-start.4 = (bf16[3,3,1536]{2,1,0:T(4,128)(2,1)S(1)}, bf16[3,3,1536]{2,1,0:T(4,128)(2,1)}, u32[]{:S(2)}) copy-start(bf16[3,3,1536]{2,1,0:T(4,128)(2,1)} %param.18) | copy-start | bytes 82948
  208.2 44.5 %all-to-all-start.1 = ((bf16[32,2,512]{2,1,0:T(2,128)(2,1)}), bf16[32,2,512]{2,1,0:T(2,128)(2,1)S(1)}, u32[]{:S(2)}, u32[]{:S(2)}) async-start(bf16[32,2,512]{2,1,0:T(2,128)(2,1)} %reshape.339), calls=%async_computation.1 | async-start | bytes 131072 | tf_op jit(solution)/shard_map/all_to_all | solution.py:18
  233.4 745.2 %all-gather.5.cloned.1.call-start = ((), (), s32[]{:S(2)}) async-start(), calls=%async_computation.8 | async-start | bytes 2162688 | tf_op jit(solution)/shard_map/all_gather | solution.py:97
  253.6 966.1 %reduce-scatter.5.cloned.1.call-start = ((), (), s32[]{:S(2)}) async-start(), calls=%async_computation.9 | async-start | bytes 7864320 | tf_op jit(solution)/shard_map/reduce_scatter | solution.py:153
  408.6 3.8 copy-start.2
  969.2 3.6 copy-start.7
  986.8 0.7 copy-start.6
  989.3 54.2 %all-to-all-start.2 = ((s32[32,1,1]{2,1,0:T(1,128)}), s32[32,1,1]{2,1,0:T(1,128)S(1)}, u32[]{:S(2)}, u32[]{:S(2)}) async-start(s32[32,1,1]{2,1,0:T(1,128)} %copy.135), calls=%async_computation.4 | async-start | bytes 32768 | tf_op jit(solution)/shard_map/all_to_all | solution.py:189
  1043.5 149.6 %all-to-all-start.3 = ((bf16[32,128,2,512]{3,1,2,0:T(8,128)(2,1)}), bf16[32,128,2,512]{3,1,2,0:T(8,128)(2,1)}, u32[]{:S(2)}, u32[]{:S(2)}) async-start(bf16[32,128,2,512]{3,1,2,0:T(8,128)(2,1)} %scatter_fusion), calls=%async_computation.5 | async-start | bytes 16777216 | tf_op jit(solution)/shard_map/all_to_all | solution.py:188
  1195.2 24.5 %copy-start.1 = (bf16[1536,512]{1,0:T(8,128)(2,1)S(1)}, bf16[1536,512]{1,0:T(8,128)(2,1)}, u32[]{:S(2)}) copy-start(bf16[1536,512]{1,0:T(8,128)(2,1)} %param.13) | copy-start | bytes 4718596
Sparse Core Ops, SparseCore 0:
  26.2 144.5 all-gather.2
  205.2 164.0 reduce-scatter.2
  371.7 135.9 all-gather.4
  987.0 64.7 reduce-scatter.4
